TPU v7x, 32 devices: a whole 2x2x4 slice. The times are simulated.
32 devices in a mesh: seq: 8 (over z, x), dp: 4 (over y, core), grp: 1.
Axes of the slice: x: 2, y: 2, z: 4, core: 2. Of those that a mesh axis runs over, the one named last changes fastest.
Arguments:
- video_queries: bfloat16 [4, 1024, 4096], P('dp', 'seq', 'grp'), may hold values from -13.5 to 13.5
- caption_keys: bfloat16 [4, 512, 4096], P('dp', 'seq', 'grp'), may hold values from -6 to 6
- caption_values: bfloat16 [4, 512, 4096], P('dp', 'seq', 'grp'), may hold values from -6 to 6
- out_grad: bfloat16 [4, 1024, 4096], P('dp', 'seq', 'grp'), may hold values from -6 to 6
- head_gate: float32 [32], replicated, may hold values from 0.25 to 2
- video_len: int32 [4], P('dp'), may hold values from 1 to 1024, 2048 in all
- cap_len: int32 [4], P('dp'), may hold values from 1 to 512, 1024 in all
Outputs:
- attended: bfloat16 [4, 1024, 4096], P('dp', 'seq', 'grp')
- query_grad: bfloat16 [4, 1024, 4096], P('dp', 'seq', 'grp')
- key_grad: bfloat16 [4, 512, 4096], P('dp', 'seq', 'grp')
- value_grad: bfloat16 [4, 512, 4096], P('dp', 'seq', 'grp')
- gate_grad: float32 [32], replicated
All inputs are finite; a program needn't handle non-finite values. No bound on the sum of `video_len` or of `cap_len` on one device may be relied on, other than what follows from the above.
Results may differ from a plain program's by a relative error of at most 0.017.
Values may be sent and summed in bfloat16 or wider, within the bound.
A program may use at most 64 MiB of HBM per device.

v0:
```python
import jax
import jax.numpy as jnp
from jax import lax
from jax.sharding import PartitionSpec as P


def compute(query_blocks, cotangent, cap_keys, values, key_live, row_live, gates):
    blocks, row_count, columns = query_blocks.shape
    captions = cap_keys.shape[0]
    head_count = gates.shape[0]
    head_width = columns // head_count
    score_scale = head_width ** (-0.5)
    query_heads = query_blocks.reshape(blocks, row_count, head_count, head_width)
    key_heads = cap_keys.reshape(captions, head_count, head_width)
    value_heads = values.reshape(captions, head_count, head_width)
    scores = (
        jnp.einsum("bthd,jhd->bhtj", query_heads, key_heads, preferred_element_type=jnp.float32)
        * score_scale
    )
    scores = jnp.where(key_live[None, None, None, :], scores, -jnp.inf)
    shifted = jnp.exp(scores - jnp.max(scores, axis=-1, keepdims=True))
    weights = shifted / jnp.sum(shifted, axis=-1, keepdims=True)
    weights_low = weights.astype(jnp.bfloat16)
    attention = jnp.einsum(
        "bhtj,jhd->bthd", weights_low, value_heads, preferred_element_type=jnp.float32
    )
    live_rows = row_live[:, :, None, None]
    head_scale = gates[None, None, :, None]
    attended = (
        (attention * head_scale * live_rows)
        .astype(jnp.bfloat16)
        .reshape(blocks * row_count, columns)
    )
    cot_heads = cotangent.reshape(blocks, row_count, head_count, head_width).astype(jnp.float32)
    gate_term = jnp.sum(cot_heads * attention * live_rows, axis=(0, 1, 3))
    grad_attention = (cot_heads * head_scale * live_rows).astype(jnp.bfloat16)
    grad_weights = jnp.einsum(
        "bthd,jhd->bhtj", grad_attention, value_heads, preferred_element_type=jnp.float32
    )
    row_delta = jnp.sum(weights * grad_weights, axis=-1, keepdims=True)
    grad_scores = (weights * (grad_weights - row_delta) * score_scale).astype(jnp.bfloat16)
    query_grad = jnp.einsum(
        "bhtj,jhd->bthd", grad_scores, key_heads, preferred_element_type=jnp.float32
    )
    query_grad = query_grad.astype(jnp.bfloat16).reshape(blocks * row_count, columns)
    key_blocks = jnp.einsum(
        "bhtj,bthd->bjhd", grad_scores, query_heads, preferred_element_type=jnp.float32
    )
    value_blocks = jnp.einsum(
        "bhtj,bthd->bjhd", weights_low, grad_attention, preferred_element_type=jnp.float32
    )
    key_blocks = lax.optimization_barrier(key_blocks.astype(jnp.bfloat16)).astype(jnp.float32)
    value_blocks = lax.optimization_barrier(value_blocks.astype(jnp.bfloat16)).astype(jnp.float32)
    key_part = jnp.sum(key_blocks, axis=0).reshape(captions, columns)
    value_part = jnp.sum(value_blocks, axis=0).reshape(captions, columns)
    return (attended, query_grad, key_part, value_part, gate_term)


def per_device(
    video_queries, caption_keys, caption_values, out_grad, head_gate, video_len, cap_len
):
    row_count = video_queries.shape[1]
    local_width = video_queries.shape[2]
    head_count = head_gate.shape[0]
    seq_count = lax.axis_size("seq")
    grp_count = lax.axis_size("grp")
    seq_index = lax.axis_index("seq")
    grp_index = lax.axis_index("grp")
    local_heads = head_count // grp_count
    head_start = grp_index * local_heads
    columns = local_width // seq_count
    group_heads = local_heads // seq_count
    mine_queries, mine_cot = (
        lax.all_to_all(video_queries[0], "seq", split_axis=1, concat_axis=0, tiled=True),
        lax.all_to_all(out_grad[0], "seq", split_axis=1, concat_axis=0, tiled=True),
    )
    keys_all, values_all = (
        lax.all_to_all(caption_keys[0], "seq", split_axis=1, concat_axis=0, tiled=True),
        lax.all_to_all(caption_values[0], "seq", split_axis=1, concat_axis=0, tiled=True),
    )
    captions = keys_all.shape[0]
    row_index = (
        jnp.arange(seq_count, dtype=jnp.int32)[:, None] * row_count
        + jnp.arange(row_count, dtype=jnp.int32)[None, :]
    )
    row_live = (row_index < video_len[0]).astype(jnp.float32)
    key_live = jnp.arange(captions, dtype=jnp.int32) < cap_len[0]
    gate_start = head_start + seq_index * group_heads
    gates = lax.dynamic_slice_in_dim(head_gate, gate_start, group_heads)
    query_blocks = mine_queries.reshape(seq_count, row_count, columns)
    cot_blocks = mine_cot.reshape(seq_count, row_count, columns)
    results = compute(query_blocks, cot_blocks, keys_all, values_all, key_live, row_live, gates)
    attended, query_grad, key_part, value_part, gate_term = results
    attended_rows, query_rows = (
        lax.all_to_all(attended, "seq", split_axis=0, concat_axis=1, tiled=True),
        lax.all_to_all(query_grad, "seq", split_axis=0, concat_axis=1, tiled=True),
    )
    key_rows, value_rows = (
        lax.all_to_all(
            key_part.astype(jnp.bfloat16), "seq", split_axis=0, concat_axis=1, tiled=True
        ),
        lax.all_to_all(
            value_part.astype(jnp.bfloat16), "seq", split_axis=0, concat_axis=1, tiled=True
        ),
    )
    gate_full = lax.dynamic_update_slice(
        jnp.zeros((head_count,), jnp.float32), gate_term, (gate_start,)
    )
    outputs = (attended_rows[None], query_rows[None], key_rows[None], value_rows[None])
    gate_grad = lax.psum(gate_full, ("seq", "dp", "grp"))
    return (outputs[0], outputs[1], outputs[2], outputs[3], gate_grad)


def solution(mesh):
    in_specs = (
        P("dp", "seq", "grp"),
        P("dp", "seq", "grp"),
        P("dp", "seq", "grp"),
        P("dp", "seq", "grp"),
        P(),
        P("dp"),
        P("dp"),
    )
    out_specs = (
        P("dp", "seq", "grp"),
        P("dp", "seq", "grp"),
        P("dp", "seq", "grp"),
        P("dp", "seq", "grp"),
        P(),
    )
    return jax.shard_map(
        per_device, mesh=mesh, in_specs=in_specs, out_specs=out_specs, check_vma=False
    )
```

profile of v0, /device:TPU:0, one launch (start us, length us, event | category | flops | bytes accessed | tf_op | source)
XLA Modules:
  0.0 249.1 jit_solution(871145652880503635)
XLA Ops:
  2.9 7.3 %all-to-all-start = ((bf16[64,8,512]{2,0,1:T(8,128)(2,1)}), bf16[64,8,512]{2,0,1:T(8,128)(2,1)S(1)}, u32[]{:S(2)}, u32[]{:S(2)}) async-start(bf16[64,8,512]{2,0,1:T(8,128)(2,1)} %copy.71), calls=%async_computation | async-start | bytes 1048576 | tf_op jit(solution)/shard_map/all_to_all | solution.py:78
  12.4 12.3 %all-to-all-done = bf16[64,8,512]{2,0,1:T(8,128)(2,1)S(1)} async-done(((bf16[64,8,512]{2,0,1:T(8,128)(2,1)}), bf16[64,8,512]{2,0,1:T(8,128)(2,1)S(1)}, u32[]{:S(2)}, u32[]{:S(2)}) %all-to-all-start) | async-done | bytes 524320 | tf_op jit(solution)/shard_map/all_to_all | solution.py:78
  24.7 3.6 %all-to-all-start.2 = ((bf16[64,8,512]{2,0,1:T(8,128)(2,1)}), bf16[64,8,512]{2,0,1:T(8,128)(2,1)S(1)}, u32[]{:S(2)}, u32[]{:S(2)}) async-start(bf16[64,8,512]{2,0,1:T(8,128)(2,1)} %copy.75), calls=%async_computation.2 | async-start | bytes 1048576 | tf_op jit(solution)/shard_map/all_to_all | solution.py:79
  30.6 12.4 %all-to-all-done.2 = bf16[64,8,512]{2,0,1:T(8,128)(2,1)S(1)} async-done(((bf16[64,8,512]{2,0,1:T(8,128)(2,1)}), bf16[64,8,512]{2,0,1:T(8,128)(2,1)S(1)}, u32[]{:S(2)}, u32[]{:S(2)}) %all-to-all-start.2) | async-done | bytes 524320 | tf_op jit(solution)/shard_map/all_to_all | solution.py:79
  43.0 3.6 %all-to-all-start.1 = ((bf16[128,8,512]{0,2,1:T(8,128)(2,1)}), bf16[128,8,512]{0,2,1:T(8,128)(2,1)S(1)}, u32[]{:S(2)}, u32[]{:S(2)}) async-start(bf16[128,8,512]{0,2,1:T(8,128)(2,1)} %bitcast.3), calls=%async_computation.1 | async-start | bytes 2097152 | tf_op jit(solution)/shard_map/all_to_all | solution.py:74
  50.0 22.6 %all-to-all-done.1 = bf16[128,8,512]{0,2,1:T(8,128)(2,1)S(1)} async-done(((bf16[128,8,512]{0,2,1:T(8,128)(2,1)}), bf16[128,8,512]{0,2,1:T(8,128)(2,1)S(1)}, u32[]{:S(2)}, u32[]{:S(2)}) %all-to-all-start.1) | async-done | bytes 1048608 | tf_op jit(solution)/shard_map/all_to_all | solution.py:74
  72.6 3.7 %all-to-all-start.4 = ((bf16[128,8,512]{0,2,1:T(8,128)(2,1)}), bf16[128,8,512]{0,2,1:T(8,128)(2,1)S(1)}, u32[]{:S(2)}, u32[]{:S(2)}) async-start(bf16[128,8,512]{0,2,1:T(8,128)(2,1)} %bitcast.86), calls=%async_computation.4 | async-start | bytes 2097152 | tf_op jit(solution)/shard_map/all_to_all | solution.py:75
  77.6 3.9 %fusion.44 = (f32[8,4,128]{2,0,1:T(8,128)S(1)}, f32[8,4,128,512]{2,3,0,1:T(8,128)S(1)}) fusion(f32[4,512,8,128]{3,1,2,0:T(8,128)S(1)} %fusion.26, pred[512]{0:T(512)(128)(4,1)S(1)} %iota_compare_fusion), kind=kOutput, calls=%fused_computation.48 | output fusion | flops 12583423 | bytes 16794112 | tf_op jit(solution)/shard_map/sub | solution.py:21
  81.5 3.2 %copy-done = f32[8,4,128,512]{2,3,0,1:T(8,128)} copy-done((f32[8,4,128,512]{2,3,0,1:T(8,128)}, f32[8,4,128,512]{2,3,0,1:T(8,128)S(1)}, u32[]{:S(2)}) %copy-start) | copy-done | bytes 8388632
  84.7 3.0 %fusion.43 = bf16[8,4,128,512]{2,3,0,1:T(8,128)(2,1)} fusion(f32[8,4,128,512]{2,3,0,1:T(8,128)S(1)} %get-tuple-element.24, f32[8,4,128]{2,0,1:T(8,128)S(1)} %get-tuple-element.23), kind=kLoop, calls=%fused_computation.47 | loop fusion | flops 4194304 | bytes 12599296 | tf_op jit(solution)/shard_map/convert_element_type | solution.py:23
  87.7 14.5 %all-to-all-done.4 = bf16[128,8,512]{0,2,1:T(8,128)(2,1)S(1)} async-done(((bf16[128,8,512]{0,2,1:T(8,128)(2,1)}), bf16[128,8,512]{0,2,1:T(8,128)(2,1)S(1)}, u32[]{:S(2)}, u32[]{:S(2)}) %all-to-all-start.4) | async-done | bytes 1048608 | tf_op jit(solution)/shard_map/all_to_all | solution.py:75
  102.3 4.3 %fusion.24 = (f32[4]{0:T(128)S(1)}, bf16[8,128,4,128]{1,3,0,2:T(8,128)(2,1)S(1)}, bf16[8,128,4,128]{1,3,0,2:T(8,128)(2,1)}) fusion(f32[8,128,4,128]{1,3,2,0:T(8,128)S(1)} %bitcast.83, f32[8,128]{1,0:T(8,128)S(1)} %fusion.40, f32[4]{0:T(128)S(1)} %dynamic_slice.3, bf16[8,4,128,512]{2,3,0,1:T(8,128)(2,1)} %fusion.43, bf16[512,4,128,1]{2,1,0,3:T(4,128)(2,1)S(1)} %bitcast.89), kind=kOutput, calls=%fused_computation.28 | convolution fusion | flops 541589504 | bytes 8917024 | tf_op jit(solution)/shard_map/bhtj,jhd->bthd/dot_general | solution.py:24
  106.6 9.8 %fusion.4 = bf16[8,4,128,512]{2,3,0,1:T(8,128)(2,1)} fusion(bf16[8,128,4,128]{1,3,0,2:T(8,128)(2,1)S(1)} %get-tuple-element.21, bf16[512,4,128,1]{2,1,0,3:T(4,128)(2,1)S(1)} %bitcast.90, f32[8,4,128,512]{2,3,0,1:T(8,128)} %copy-done, f32[8,4,128]{2,0,1:T(8,128)S(1)} %get-tuple-element.23), kind=kOutput, calls=%fused_computation.6 | convolution fusion | flops 1088426496 | bytes 14172160 | tf_op jit(solution)/shard_map/sub | solution.py:41
  116.4 5.4 %convert_bitcast_fusion.1 = bf16[8,512,4,128]{3,1,2,0:T(8,128)(2,1)} fusion(bf16[8,128,4,128]{1,3,2,0:T(8,128)(2,1)S(1)} %bitcast.85, bf16[8,4,128,512]{2,3,0,1:T(8,128)(2,1)} %fusion.4), kind=kOutput, calls=%fused_computation.17 | convolution fusion | flops 538968064 | bytes 9437184 | tf_op jit(solution)/shard_map/bhtj,bthd->bjhd/dot_general | solution.py:46
  126.0 3.7 %all-to-all-start.6 = ((bf16[8,64,512]{2,1,0:T(8,128)(2,1)}), bf16[8,64,512]{2,1,0:T(8,128)(2,1)S(1)}, u32[]{:S(2)}, u32[]{:S(2)}) async-start(bf16[8,64,512]{2,1,0:T(8,128)(2,1)} %convert_element_type.70), calls=%async_computation.6 | async-start | bytes 1048576 | tf_op jit(solution)/shard_map/all_to_all | solution.py:99
  129.8 5.4 %convert_bitcast_fusion = bf16[8,512,4,128]{1,3,2,0:T(8,128)(2,1)} fusion(bf16[8,4,128,512]{2,3,0,1:T(8,128)(2,1)} %fusion.43, bf16[8,128,4,128]{1,3,0,2:T(8,128)(2,1)S(1)} %get-tuple-element.21), kind=kOutput, calls=%fused_computation.16 | convolution fusion | flops 538968064 | bytes 9437184 | tf_op jit(solution)/shard_map/bhtj,bthd->bjhd/dot_general | solution.py:49
  139.3 5.0 %all-to-all-done.6 = bf16[8,64,512]{2,1,0:T(8,128)(2,1)S(1)} async-done(((bf16[8,64,512]{2,1,0:T(8,128)(2,1)}), bf16[8,64,512]{2,1,0:T(8,128)(2,1)S(1)}, u32[]{:S(2)}, u32[]{:S(2)}) %all-to-all-start.6) | async-done | bytes 524320 | tf_op jit(solution)/shard_map/all_to_all | solution.py:99
  144.3 3.6 %all-to-all-start.7 = ((bf16[8,64,512]{2,1,0:T(8,128)(2,1)}), bf16[8,64,512]{2,1,0:T(8,128)(2,1)S(1)}, u32[]{:S(2)}, u32[]{:S(2)}) async-start(bf16[8,64,512]{2,1,0:T(8,128)(2,1)} %convert_element_type.73), calls=%async_computation.7 | async-start | bytes 1048576 | tf_op jit(solution)/shard_map/all_to_all | solution.py:102
  148.0 2.9 %fusion.25 = bf16[8,128,4,128]{1,3,0,2:T(8,128)(2,1)S(1)} fusion(bf16[512,4,128,1]{0,2,3,1:T(8,128)(2,1)S(1)} %copy.106, bf16[8,4,128,512]{2,3,0,1:T(8,128)(2,1)} %fusion.4), kind=kOutput, calls=%fused_computation.31 | convolution fusion | flops 537395200 | bytes 5767168 | tf_op jit(solution)/shard_map/bhtj,jhd->bthd/dot_general | solution.py:42
  152.0 10.7 %all-to-all-done.7 = bf16[8,64,512]{2,1,0:T(8,128)(2,1)S(1)} async-done(((bf16[8,64,512]{2,1,0:T(8,128)(2,1)}), bf16[8,64,512]{2,1,0:T(8,128)(2,1)S(1)}, u32[]{:S(2)}, u32[]{:S(2)}) %all-to-all-start.7) | async-done | bytes 524320 | tf_op jit(solution)/shard_map/all_to_all | solution.py:102
  162.6 3.6 %all-to-all-start.5 = ((bf16[8,128,512]{1,2,0:T(8,128)(2,1)}), bf16[8,128,512]{1,2,0:T(8,128)(2,1)S(1)}, u32[]{:S(2)}, u32[]{:S(2)}) async-start(bf16[8,128,512]{1,2,0:T(8,128)(2,1)} %bitcast.21), calls=%async_computation.5 | async-start | bytes 2097152 | tf_op jit(solution)/shard_map/all_to_all | solution.py:96
  167.3 24.9 %all-to-all-done.5 = bf16[8,128,512]{1,2,0:T(8,128)(2,1)S(1)} async-done(((bf16[8,128,512]{1,2,0:T(8,128)(2,1)}), bf16[8,128,512]{1,2,0:T(8,128)(2,1)S(1)}, u32[]{:S(2)}, u32[]{:S(2)}) %all-to-all-start.5) | async-done | bytes 1048608 | tf_op jit(solution)/shard_map/all_to_all | solution.py:96
  192.2 3.6 %all-to-all-start.3 = ((bf16[8,128,512]{1,2,0:T(8,128)(2,1)}), bf16[8,128,512]{1,2,0:T(8,128)(2,1)S(1)}, u32[]{:S(2)}, u32[]{:S(2)}) async-start(bf16[8,128,512]{1,2,0:T(8,128)(2,1)} %bitcast.11), calls=%async_computation.3 | async-start | bytes 2097152 | tf_op jit(solution)/shard_map/all_to_all | solution.py:95
  196.1 45.9 %psum.7 = f32[32]{0:T(128)} all-reduce(f32[32]{0:T(128)S(1)} %dynamic_update_slice.3), channel_id=1, replica_groups=mesh['seq'=8,'dp'=4,'grp'=1] {'seq','dp','grp'}, use_global_device_ids=true, to_apply=%region_6.7 | all-reduce | flops 32 | bytes 256 | tf_op jit(solution)/shard_map/psum | solution.py:110
  (39 shorter events, 28.0 us)
Async XLA Ops:
  0.6 46.6 %copy-start.2 = (bf16[1,128,4096]{2,1,0:T(8,128)(2,1)S(1)}, bf16[1,128,4096]{2,1,0:T(8,128)(2,1)}, u32[]{:S(2)}) copy-start(bf16[1,128,4096]{2,1,0:T(8,128)(2,1)} %param.10) | copy-start | bytes 3145732
  0.6 48.6 %copy-start.3 = (f32[32]{0:T(128)S(1)}, f32[32]{0:T(128)}, u32[]{:S(2)}) copy-start(f32[32]{0:T(128)} %param.11) | copy-start | bytes 388
  2.9 21.8 %all-to-all-start = ((bf16[64,8,512]{2,0,1:T(8,128)(2,1)}), bf16[64,8,512]{2,0,1:T(8,128)(2,1)S(1)}, u32[]{:S(2)}, u32[]{:S(2)}) async-start(bf16[64,8,512]{2,0,1:T(8,128)(2,1)} %copy.71), calls=%async_computation | async-start | bytes 1048576 | tf_op jit(solution)/shard_map/all_to_all | solution.py:78
  24.7 18.3 %all-to-all-start.2 = ((bf16[64,8,512]{2,0,1:T(8,128)(2,1)}), bf16[64,8,512]{2,0,1:T(8,128)(2,1)S(1)}, u32[]{:S(2)}, u32[]{:S(2)}) async-start(bf16[64,8,512]{2,0,1:T(8,128)(2,1)} %copy.75), calls=%async_computation.2 | async-start | bytes 1048576 | tf_op jit(solution)/shard_map/all_to_all | solution.py:79
  43.0 29.6 %all-to-all-start.1 = ((bf16[128,8,512]{0,2,1:T(8,128)(2,1)}), bf16[128,8,512]{0,2,1:T(8,128)(2,1)S(1)}, u32[]{:S(2)}, u32[]{:S(2)}) async-start(bf16[128,8,512]{0,2,1:T(8,128)(2,1)} %bitcast.3), calls=%async_computation.1 | async-start | bytes 2097152 | tf_op jit(solution)/shard_map/all_to_all | solution.py:74
  72.6 29.6 %all-to-all-start.4 = ((bf16[128,8,512]{0,2,1:T(8,128)(2,1)}), bf16[128,8,512]{0,2,1:T(8,128)(2,1)S(1)}, u32[]{:S(2)}, u32[]{:S(2)}) async-start(bf16[128,8,512]{0,2,1:T(8,128)(2,1)} %bitcast.86), calls=%async_computation.4 | async-start | bytes 2097152 | tf_op jit(solution)/shard_map/all_to_all | solution.py:75
  81.5 3.2 %copy-start = (f32[8,4,128,512]{2,3,0,1:T(8,128)}, f32[8,4,128,512]{2,3,0,1:T(8,128)S(1)}, u32[]{:S(2)}) copy-start(f32[8,4,128,512]{2,3,0,1:T(8,128)S(1)} %get-tuple-element.24) | copy-start | bytes 25165828
  126.0 18.3 %all-to-all-start.6 = ((bf16[8,64,512]{2,1,0:T(8,128)(2,1)}), bf16[8,64,512]{2,1,0:T(8,128)(2,1)S(1)}, u32[]{:S(2)}, u32[]{:S(2)}) async-start(bf16[8,64,512]{2,1,0:T(8,128)(2,1)} %convert_element_type.70), calls=%async_computation.6 | async-start | bytes 1048576 | tf_op jit(solution)/shard_map/all_to_all | solution.py:99
  138.0 28.3 %copy-start.1 = (bf16[8,128,4,128]{1,3,0,2:T(8,128)(2,1)S(1)}, bf16[8,128,4,128]{1,3,0,2:T(8,128)(2,1)}, u32[]{:S(2)}) copy-start(bf16[8,128,4,128]{1,3,0,2:T(8,128)(2,1)} %get-tuple-element.22) | copy-start | bytes 3145732
  144.3 18.3 %all-to-all-start.7 = ((bf16[8,64,512]{2,1,0:T(8,128)(2,1)}), bf16[8,64,512]{2,1,0:T(8,128)(2,1)S(1)}, u32[]{:S(2)}, u32[]{:S(2)}) async-start(bf16[8,64,512]{2,1,0:T(8,128)(2,1)} %convert_element_type.73), calls=%async_computation.7 | async-start | bytes 1048576 | tf_op jit(solution)/shard_map/all_to_all | solution.py:102
  162.6 29.6 %all-to-all-start.5 = ((bf16[8,128,512]{1,2,0:T(8,128)(2,1)}), bf16[8,128,512]{1,2,0:T(8,128)(2,1)S(1)}, u32[]{:S(2)}, u32[]{:S(2)}) async-start(bf16[8,128,512]{1,2,0:T(8,128)(2,1)} %bitcast.21), calls=%async_computation.5 | async-start | bytes 2097152 | tf_op jit(solution)/shard_map/all_to_all | solution.py:96
  192.2 55.6 %all-to-all-start.3 = ((bf16[8,128,512]{1,2,0:T(8,128)(2,1)}), bf16[8,128,512]{1,2,0:T(8,128)(2,1)S(1)}, u32[]{:S(2)}, u32[]{:S(2)}) async-start(bf16[8,128,512]{1,2,0:T(8,128)(2,1)} %bitcast.11), calls=%async_computation.3 | async-start | bytes 2097152 | tf_op jit(solution)/shard_map/all_to_all | solution.py:95
where the time goes:
time: 250 us; the launch traced here: 249 us
  waiting for transfers between devices  102 us (41%)
  blocking collectives  45.9 us (18%)
  starting transfers between devices  32.9 us (13%)
  matrix products  29.1 us (12%)
  local copies, waits for them, and re-layouts  24 us (10%)
  other arithmetic  12.8 us (5%)
    psum x1, blocking collectives, per_device(): gate_grad = lax.psum(gate_full, ('seq', 'dp', 'grp'))  45.9 us
    all_to_all x1, waiting for transfers between devices, per_device(): lax.all_to_all(query_grad, 'seq', split_axis=0, concat_axis=1, tiled=True)  24.9 us
    all_to_all x1, waiting for transfers between devices, per_device(): lax.all_to_all(video_queries[0], 'seq', split_axis=1, concat_axis=0, tile...  22.6 us
    all_to_all x1, waiting for transfers between devices, per_device(): lax.all_to_all(out_grad[0], 'seq', split_axis=1, concat_axis=0, tiled=True)  14.5 us
    all_to_all x1, waiting for transfers between devices, per_device(): lax.all_to_all(caption_values[0], 'seq', split_axis=1, concat_axis=0, til...  12.4 us
    all_to_all x1, waiting for transfers between devices, per_device(): lax.all_to_all(caption_keys[0], 'seq', split_axis=1, concat_axis=0, tiled...  12.3 us
    unnamed x14, local copies, waits for them, and re-layouts  11.9 us
    all_to_all x1, waiting for transfers between devices, per_device(): lax.all_to_all(value_part.astype(jnp.bfloat16), 'seq', split_axis=0, conc...  10.7 us
  transfers between devices with their start and end apart: 8, of which 7 were waited for; matrix products, arithmetic and copies ran while one was open for 14% of the time, Pallas kernels for 0%

commit v1 on v0

--- a/solution.py
+++ b/solution.py
@@ -2,6 +2,28 @@
 import jax.numpy as jnp
 from jax import lax
 from jax.sharding import PartitionSpec as P
+
+
+def cut_along(shard, dim, peers):
+    before, after = (shard.shape[:dim], shard.shape[dim + 1 :])
+    return jnp.moveaxis(shard.reshape(*before, peers, -1, *after), dim, 0)
+
+
+def laid_out(pieces, dim):
+    shape = list(pieces.shape[1:])
+    shape[dim] *= pieces.shape[0]
+    return jnp.moveaxis(pieces, 0, dim).reshape(shape)
+
+
+def exchange_in_pairs(x, axis, split_dim, concat_dim):
+    size, mine = (lax.axis_size(axis), lax.axis_index(axis))
+    parts = cut_along(x, split_dim, size)
+    outs = [parts[mine]]
+    for step in range(1, size):
+        sent = parts[mine ^ step]
+        outs.append(lax.ppermute(sent, axis, [(i, i ^ step) for i in range(size)]))
+    parts = jnp.stack(outs)[mine ^ jnp.arange(size)]
+    return laid_out(parts, concat_dim)
 
 
 def compute(query_blocks, cotangent, cap_keys, values, key_live, row_live, gates):
@@ -76,7 +98,7 @@
     )
     keys_all, values_all = (
         lax.all_to_all(caption_keys[0], "seq", split_axis=1, concat_axis=0, tiled=True),
-        lax.all_to_all(caption_values[0], "seq", split_axis=1, concat_axis=0, tiled=True),
+        exchange_in_pairs(caption_values[0], "seq", 1, 0),
     )
     captions = keys_all.shape[0]
     row_index = (

time: 250 us -> 235 us (0.940)
  waiting for transfers between devices: 102 us -> 64.2 us
  starting transfers between devices: 32.9 us -> 46.7 us
  local copies, waits for them, and re-layouts: 24 us -> 33.7 us
    all_to_all x1, waiting for transfers between devices: 22.6 us -> 4.17 us  [per_device(): lax.all_to_all(video_queries[0], 'seq', split_axis=1, concat_axis=0, tile...]
    ppermute x0 -> x7, starting transfers between devices: none -> 13.2 us  [exchange_in_pairs(): outs.append(lax.ppermute(sent, axis, [(i, i ^ step) for i in range(size)]))]
    all_to_all x1 -> x0, waiting for transfers between devices: 12.4 us -> none  [per_device(): lax.all_to_all(caption_values[0], 'seq', split_axis=1, concat_axis=0, til...]
    all_to_all x1, waiting for transfers between devices: 10.7 us -> 0.01 us  [per_device(): lax.all_to_all(value_part.astype(jnp.bfloat16), 'seq', split_axis=0, conc...]
    ppermute x0 -> x7, waiting for transfers between devices: none -> 9.95 us  [exchange_in_pairs(): outs.append(lax.ppermute(sent, axis, [(i, i ^ step) for i in range(size)]))]
    all_to_all x1, waiting for transfers between devices: 12.3 us -> 3.26 us  [per_device(): lax.all_to_all(caption_keys[0], 'seq', split_axis=1, concat_axis=0, tiled...]
    unnamed x14 -> x30, local copies, waits for them, and re-layouts: 11.9 us -> 18.8 us
    all_to_all x1, waiting for transfers between devices: 4.99 us -> 9.45 us  [per_device(): lax.all_to_all(key_part.astype(jnp.bfloat16), 'seq', split_axis=0, concat...]
  transfers between devices with their start and end apart: 8 -> 14, of which waited for: 7 -> 7; matrix products, arithmetic and copies ran while one was open for 14% -> 22% of each run, Pallas kernels for 0% -> 0%
where the time goes in v1:
time: 235 us; the launch traced here: 233 us
  waiting for transfers between devices  64.2 us (27%)
  starting transfers between devices  46.7 us (20%)
  blocking collectives  45.7 us (19%)
  local copies, waits for them, and re-layouts  33.7 us (14%)
  matrix products  27.2 us (12%)
  other arithmetic  13.7 us (6%)
    psum x1, blocking collectives, per_device(): gate_grad = lax.psum(gate_full, ('seq', 'dp', 'grp'))  45.7 us
    all_to_all x1, waiting for transfers between devices, per_device(): lax.all_to_all(query_grad, 'seq', split_axis=0, concat_axis=1, tiled=True)  24.2 us
    unnamed x30, local copies, waits for them, and re-layouts  18.8 us
    ppermute x7, starting transfers between devices, exchange_in_pairs(): outs.append(lax.ppermute(sent, axis, [(i, i ^ step) for i in range(size)]))  13.2 us
    all_to_all x1, waiting for transfers between devices, per_device(): lax.all_to_all(out_grad[0], 'seq', split_axis=1, concat_axis=0, tiled=True)  13.2 us
    ppermute x7, waiting for transfers between devices, exchange_in_pairs(): outs.append(lax.ppermute(sent, axis, [(i, i ^ step) for i in range(size)]))  9.95 us
    sub x1, matrix products, compute(): grad_weights - row_delta  9.91 us
    all_to_all x1, waiting for transfers between devices, per_device(): lax.all_to_all(key_part.astype(jnp.bfloat16), 'seq', split_axis=0, concat...  9.45 us
  transfers between devices with their start and end apart: 14, of which 7 were waited for; matrix products, arithmetic and copies ran while one was open for 22% of the time, Pallas kernels for 0%

profile of v1, /device:TPU:0, one launch (start us, length us, event | category | flops | bytes accessed | tf_op | source)
XLA Modules:
  0.0 233.4 jit_solution(7313652531205831764)
XLA Ops:
  2.9 7.3 %all-to-all-start = ((bf16[64,8,512]{2,0,1:T(8,128)(2,1)}), bf16[64,8,512]{2,0,1:T(8,128)(2,1)S(1)}, u32[]{:S(2)}, u32[]{:S(2)}) async-start(bf16[64,8,512]{2,0,1:T(8,128)(2,1)} %copy.65), calls=%async_computation | async-start | bytes 1048576 | tf_op jit(solution)/shard_map/all_to_all | solution.py:100
  18.1 3.0 %collective-permute-start.3 = (bf16[64,512]{1,0:T(8,128)(2,1)S(1)}, bf16[64,512]{1,0:T(8,128)(2,1)}, u32[]{:S(2)}, u32[]{:S(2)}) collective-permute-start(bf16[64,512]{1,0:T(8,128)(2,1)S(1)} %bitcast.137), channel_id=1, source_target_pairs={{0,16},{4,20},{8,24},{12,28},{16,0},{20,4},{24,8},{28,12},{1,17},{... | collective-permute-start | bytes 196616 | tf_op jit(solution)/shard_map/ppermute | solution.py:24
  25.6 3.3 %all-to-all-done = bf16[64,8,512]{2,0,1:T(8,128)(2,1)S(1)} async-done(((bf16[64,8,512]{2,0,1:T(8,128)(2,1)}), bf16[64,8,512]{2,0,1:T(8,128)(2,1)S(1)}, u32[]{:S(2)}, u32[]{:S(2)}) %all-to-all-start) | async-done | bytes 524320 | tf_op jit(solution)/shard_map/all_to_all | solution.py:100
  28.9 3.6 %all-to-all-start.1 = ((bf16[128,8,512]{0,2,1:T(8,128)(2,1)}), bf16[128,8,512]{0,2,1:T(8,128)(2,1)S(1)}, u32[]{:S(2)}, u32[]{:S(2)}) async-start(bf16[128,8,512]{0,2,1:T(8,128)(2,1)} %bitcast.12), calls=%async_computation.1 | async-start | bytes 2097152 | tf_op jit(solution)/shard_map/all_to_all | solution.py:96
  35.2 3.8 %collective-permute-start.5 = (bf16[64,512]{1,0:T(8,128)(2,1)}, bf16[64,512]{1,0:T(8,128)(2,1)S(1)}, u32[]{:S(2)}, u32[]{:S(2)}) collective-permute-start(bf16[64,512]{1,0:T(8,128)(2,1)} %bitcast.139), channel_id=1, source_target_pairs={{0,24},{4,28},{8,16},{12,20},{16,8},{20,12},{24,0},{28,4},{1,25},{... | collective-permute-start | bytes 196616 | tf_op jit(solution)/shard_map/ppermute | solution.py:24
  44.7 8.5 %collective-permute-done.5 = bf16[64,512]{1,0:T(8,128)(2,1)S(1)} collective-permute-done((bf16[64,512]{1,0:T(8,128)(2,1)}, bf16[64,512]{1,0:T(8,128)(2,1)S(1)}, u32[]{:S(2)}, u32[]{:S(2)}) %collective-permute-start.5) | collective-permute-done | bytes 65568 | tf_op jit(solution)/shard_map/ppermute | solution.py:24
  55.8 4.2 %all-to-all-done.1 = bf16[128,8,512]{0,2,1:T(8,128)(2,1)S(1)} async-done(((bf16[128,8,512]{0,2,1:T(8,128)(2,1)}), bf16[128,8,512]{0,2,1:T(8,128)(2,1)S(1)}, u32[]{:S(2)}, u32[]{:S(2)}) %all-to-all-start.1) | async-done | bytes 1048608 | tf_op jit(solution)/shard_map/all_to_all | solution.py:96
  60.0 5.3 %all-to-all-start.3 = ((bf16[128,8,512]{0,2,1:T(8,128)(2,1)}), bf16[128,8,512]{0,2,1:T(8,128)(2,1)S(1)}, u32[]{:S(2)}, u32[]{:S(2)}) async-start(bf16[128,8,512]{0,2,1:T(8,128)(2,1)} %bitcast.125), calls=%async_computation.3 | async-start | bytes 2097152 | tf_op jit(solution)/shard_map/all_to_all | solution.py:97
  66.6 3.9 %fusion.45 = (f32[8,4,128]{2,0,1:T(8,128)S(1)}, f32[8,4,128,512]{2,3,0,1:T(8,128)S(1)}) fusion(f32[4,512,8,128]{3,1,2,0:T(8,128)S(1)} %fusion.26, pred[512]{0:T(512)(128)(4,1)S(1)} %iota_compare_fusion), kind=kOutput, calls=%fused_computation.75 | output fusion | flops 12583423 | bytes 16794112 | tf_op jit(solution)/shard_map/sub | solution.py:43
  70.5 3.2 %copy-done.1 = f32[8,4,128,512]{2,3,0,1:T(8,128)} copy-done((f32[8,4,128,512]{2,3,0,1:T(8,128)}, f32[8,4,128,512]{2,3,0,1:T(8,128)S(1)}, u32[]{:S(2)}) %copy-start.1) | copy-done | bytes 8388632
  73.7 3.0 %fusion.44 = bf16[8,4,128,512]{2,3,0,1:T(8,128)(2,1)} fusion(f32[8,4,128,512]{2,3,0,1:T(8,128)S(1)} %get-tuple-element.32, f32[8,4,128]{2,0,1:T(8,128)S(1)} %get-tuple-element.31), kind=kLoop, calls=%fused_computation.74 | loop fusion | flops 4194304 | bytes 12599296 | tf_op jit(solution)/shard_map/convert_element_type | solution.py:45
  76.7 13.2 %all-to-all-done.3 = bf16[128,8,512]{0,2,1:T(8,128)(2,1)S(1)} async-done(((bf16[128,8,512]{0,2,1:T(8,128)(2,1)}), bf16[128,8,512]{0,2,1:T(8,128)(2,1)S(1)}, u32[]{:S(2)}, u32[]{:S(2)}) %all-to-all-start.3) | async-done | bytes 1048608 | tf_op jit(solution)/shard_map/all_to_all | solution.py:97
  90.1 4.4 %fusion.24 = (f32[4]{0:T(128)S(1)}, bf16[8,128,4,128]{1,3,0,2:T(8,128)(2,1)S(1)}, bf16[8,128,4,128]{1,3,0,2:T(8,128)(2,1)}) fusion(f32[8,128,4,128]{1,3,2,0:T(8,128)S(1)} %bitcast.121, f32[8,128]{1,0:T(8,128)S(1)} %fusion.40, f32[4]{0:T(128)S(1)} %dynamic_slice.5, bf16[8,4,128,512]{2,3,0,1:T(8,128)(2,1)} %fusion.44, bf16[512,4,128,1]{2,1,0,3:T(4,128)(2,1)S(1)} %bitcast.128), kind=kOutput, calls=%fused_computation.29 | convolution fusion | flops 541589504 | bytes 8917024 | tf_op jit(solution)/shard_map/bhtj,jhd->bthd/dot_general | solution.py:46
  94.5 3.2 %convert_bitcast_fusion = bf16[8,512,4,128]{1,3,2,0:T(8,128)(2,1)} fusion(bf16[8,4,128,512]{2,3,0,1:T(8,128)(2,1)S(1)} %copy-done, bf16[8,128,4,128]{1,3,0,2:T(8,128)(2,1)S(1)} %get-tuple-element.21), kind=kOutput, calls=%fused_computation.17 | convolution fusion | flops 538968064 | bytes 9437184 | tf_op jit(solution)/shard_map/bhtj,bthd->bjhd/dot_general | solution.py:71
  97.7 3.8 %reduce_sum.54 = bf16[512,4,128]{0,2,1:T(8,128)(2,1)} reduce(bf16[8,512,4,128]{1,3,2,0:T(8,128)(2,1)} %convert_bitcast_fusion, bf16[]{:T(256)} %constant.43.clone.1), dimensions={0}, to_apply=%region_4.5 | reduce | flops 1835008 | bytes 4718594 | tf_op jit(solution)/shard_map/reduce_sum | solution.py:77
  105.6 4.4 %all-to-all-start.6 = ((bf16[8,64,512]{2,1,0:T(8,128)(2,1)}), bf16[8,64,512]{2,1,0:T(8,128)(2,1)}, u32[]{:S(2)}, u32[]{:S(2)}) async-start(bf16[8,64,512]{2,1,0:T(8,128)(2,1)} %convert_element_type.73), calls=%async_computation.6 | async-start | bytes 1048576 | tf_op jit(solution)/shard_map/all_to_all | solution.py:124
  109.9 9.9 %fusion.4 = bf16[8,4,128,512]{2,3,0,1:T(8,128)(2,1)} fusion(bf16[8,128,4,128]{1,3,0,2:T(8,128)(2,1)S(1)} %get-tuple-element.21, bf16[512,4,128,1]{2,1,0,3:T(4,128)(2,1)S(1)} %bitcast.129, f32[8,4,128,512]{2,3,0,1:T(8,128)} %copy-done.1, f32[8,4,128]{2,0,1:T(8,128)S(1)} %get-tuple-element.31), kind=kOutput, calls=%fused_computation.7 | convolution fusion | flops 1088426496 | bytes 14172160 | tf_op jit(solution)/shard_map/sub | solution.py:63
  119.9 5.4 %convert_bitcast_fusion.1 = bf16[8,512,4,128]{3,1,2,0:T(8,128)(2,1)} fusion(bf16[8,128,4,128]{1,3,2,0:T(8,128)(2,1)S(1)} %bitcast.123, bf16[8,4,128,512]{2,3,0,1:T(8,128)(2,1)} %fusion.4), kind=kOutput, calls=%fused_computation.18 | convolution fusion | flops 538968064 | bytes 9437184 | tf_op jit(solution)/shard_map/bhtj,bthd->bjhd/dot_general | solution.py:68
  129.5 5.7 %all-to-all-start.5 = ((bf16[8,64,512]{2,1,0:T(8,128)(2,1)}), bf16[8,64,512]{2,1,0:T(8,128)(2,1)S(1)}, u32[]{:S(2)}, u32[]{:S(2)}) async-start(bf16[8,64,512]{2,1,0:T(8,128)(2,1)} %convert_element_type.70), calls=%async_computation.5 | async-start | bytes 1048576 | tf_op jit(solution)/shard_map/all_to_all | solution.py:121
  139.2 9.4 %all-to-all-done.5 = bf16[8,64,512]{2,1,0:T(8,128)(2,1)S(1)} async-done(((bf16[8,64,512]{2,1,0:T(8,128)(2,1)}), bf16[8,64,512]{2,1,0:T(8,128)(2,1)S(1)}, u32[]{:S(2)}, u32[]{:S(2)}) %all-to-all-start.5) | async-done | bytes 524320 | tf_op jit(solution)/shard_map/all_to_all | solution.py:121
  148.6 3.7 %all-to-all-start.4 = ((bf16[8,128,512]{1,2,0:T(8,128)(2,1)}), bf16[8,128,512]{1,2,0:T(8,128)(2,1)S(1)}, u32[]{:S(2)}, u32[]{:S(2)}) async-start(bf16[8,128,512]{1,2,0:T(8,128)(2,1)} %bitcast.28), calls=%async_computation.4 | async-start | bytes 2097152 | tf_op jit(solution)/shard_map/all_to_all | solution.py:118
  153.4 24.2 %all-to-all-done.4 = bf16[8,128,512]{1,2,0:T(8,128)(2,1)S(1)} async-done(((bf16[8,128,512]{1,2,0:T(8,128)(2,1)}), bf16[8,128,512]{1,2,0:T(8,128)(2,1)S(1)}, u32[]{:S(2)}, u32[]{:S(2)}) %all-to-all-start.4) | async-done | bytes 1048608 | tf_op jit(solution)/shard_map/all_to_all | solution.py:118
  177.6 3.6 %all-to-all-start.2 = ((bf16[8,128,512]{1,2,0:T(8,128)(2,1)}), bf16[8,128,512]{1,2,0:T(8,128)(2,1)S(1)}, u32[]{:S(2)}, u32[]{:S(2)}) async-start(bf16[8,128,512]{1,2,0:T(8,128)(2,1)} %bitcast.18), calls=%async_computation.2 | async-start | bytes 2097152 | tf_op jit(solution)/shard_map/all_to_all | solution.py:117
  181.4 45.7 %psum.7 = f32[32]{0:T(128)} all-reduce(f32[32]{0:T(128)S(1)} %dynamic_update_slice.3), channel_id=1, replica_groups=mesh['seq'=8,'dp'=4,'grp'=1] {'seq','dp','grp'}, use_global_device_ids=true, to_apply=%region_6.7 | all-reduce | flops 32 | bytes 256 | tf_op jit(solution)/shard_map/psum | solution.py:132
  (71 shorter events, 45.7 us)
Async XLA Ops:
  0.6 33.1 %copy-start.3 = (bf16[1,128,4096]{2,1,0:T(8,128)(2,1)S(1)}, bf16[1,128,4096]{2,1,0:T(8,128)(2,1)}, u32[]{:S(2)}) copy-start(bf16[1,128,4096]{2,1,0:T(8,128)(2,1)} %param.10) | copy-start | bytes 3145732
  0.6 34.5 %copy-start.4 = (f32[32]{0:T(128)S(1)}, f32[32]{0:T(128)}, u32[]{:S(2)}) copy-start(f32[32]{0:T(128)} %param.11) | copy-start | bytes 388
  2.9 26.0 %all-to-all-start = ((bf16[64,8,512]{2,0,1:T(8,128)(2,1)}), bf16[64,8,512]{2,0,1:T(8,128)(2,1)S(1)}, u32[]{:S(2)}, u32[]{:S(2)}) async-start(bf16[64,8,512]{2,0,1:T(8,128)(2,1)} %copy.65), calls=%async_computation | async-start | bytes 1048576 | tf_op jit(solution)/shard_map/all_to_all | solution.py:100
  13.3 21.9 %collective-permute-start = (bf16[64,512]{1,0:T(8,128)(2,1)}, bf16[64,512]{1,0:T(8,128)(2,1)}, u32[]{:S(2)}, u32[]{:S(2)}) collective-permute-start(bf16[64,512]{1,0:T(8,128)(2,1)} %bitcast.118), channel_id=1, source_target_pairs={{0,4},{4,0},{8,12},{12,8},{16,20},{20,16},{24,28},{28,24},{1,5},{5... | collective-permute-start | bytes 196616 | tf_op jit(solution)/shard_map/ppermute | solution.py:24
  16.0 23.9 %collective-permute-start.1 = (bf16[64,512]{1,0:T(8,128)(2,1)}, bf16[64,512]{1,0:T(8,128)(2,1)}, u32[]{:S(2)}, u32[]{:S(2)}) collective-permute-start(bf16[64,512]{1,0:T(8,128)(2,1)} %bitcast.117), channel_id=1, source_target_pairs={{0,8},{4,12},{8,0},{12,4},{16,24},{20,28},{24,16},{28,20},{1,9},{5... | collective-permute-start | bytes 196616 | tf_op jit(solution)/shard_map/ppermute | solution.py:24
  18.1 24.1 %collective-permute-start.2 = (bf16[64,512]{1,0:T(8,128)(2,1)}, bf16[64,512]{1,0:T(8,128)(2,1)}, u32[]{:S(2)}, u32[]{:S(2)}) collective-permute-start(bf16[64,512]{1,0:T(8,128)(2,1)} %bitcast.116), channel_id=1, source_target_pairs={{0,12},{4,8},{8,4},{12,0},{16,28},{20,24},{24,20},{28,16},{1,13},{... | collective-permute-start | bytes 196616 | tf_op jit(solution)/shard_map/ppermute | solution.py:24
  18.1 24.9 %collective-permute-start.3 = (bf16[64,512]{1,0:T(8,128)(2,1)S(1)}, bf16[64,512]{1,0:T(8,128)(2,1)}, u32[]{:S(2)}, u32[]{:S(2)}) collective-permute-start(bf16[64,512]{1,0:T(8,128)(2,1)S(1)} %bitcast.137), channel_id=1, source_target_pairs={{0,16},{4,20},{8,24},{12,28},{16,0},{20,4},{24,8},{28,12},{1,17},{... | collective-permute-start | bytes 196616 | tf_op jit(solution)/shard_map/ppermute | solution.py:24
  21.1 22.7 %collective-permute-start.4 = (bf16[64,512]{1,0:T(8,128)(2,1)S(1)}, bf16[64,512]{1,0:T(8,128)(2,1)}, u32[]{:S(2)}, u32[]{:S(2)}) collective-permute-start(bf16[64,512]{1,0:T(8,128)(2,1)S(1)} %bitcast.136), channel_id=1, source_target_pairs={{0,20},{4,16},{8,28},{12,24},{16,4},{20,0},{24,12},{28,8},{1,21},{... | collective-permute-start | bytes 196616 | tf_op jit(solution)/shard_map/ppermute | solution.py:24
  28.9 31.1 %all-to-all-start.1 = ((bf16[128,8,512]{0,2,1:T(8,128)(2,1)}), bf16[128,8,512]{0,2,1:T(8,128)(2,1)S(1)}, u32[]{:S(2)}, u32[]{:S(2)}) async-start(bf16[128,8,512]{0,2,1:T(8,128)(2,1)} %bitcast.12), calls=%async_computation.1 | async-start | bytes 2097152 | tf_op jit(solution)/shard_map/all_to_all | solution.py:96
  35.2 18.0 %collective-permute-start.5 = (bf16[64,512]{1,0:T(8,128)(2,1)}, bf16[64,512]{1,0:T(8,128)(2,1)S(1)}, u32[]{:S(2)}, u32[]{:S(2)}) collective-permute-start(bf16[64,512]{1,0:T(8,128)(2,1)} %bitcast.139), channel_id=1, source_target_pairs={{0,24},{4,28},{8,16},{12,20},{16,8},{20,12},{24,0},{28,4},{1,25},{... | collective-permute-start | bytes 196616 | tf_op jit(solution)/shard_map/ppermute | solution.py:24
  39.8 14.8 %collective-permute-start.6 = (bf16[64,512]{1,0:T(8,128)(2,1)S(1)}, bf16[64,512]{1,0:T(8,128)(2,1)S(1)}, u32[]{:S(2)}, u32[]{:S(2)}) collective-permute-start(bf16[64,512]{1,0:T(8,128)(2,1)S(1)} %bitcast.138), channel_id=1, source_target_pairs={{0,28},{4,24},{8,20},{12,16},{16,12},{20,8},{24,4},{28,0},{1,29},{... | collective-permute-start | bytes 196616 | tf_op jit(solution)/shard_map/ppermute | solution.py:24
  60.0 30.0 %all-to-all-start.3 = ((bf16[128,8,512]{0,2,1:T(8,128)(2,1)}), bf16[128,8,512]{0,2,1:T(8,128)(2,1)S(1)}, u32[]{:S(2)}, u32[]{:S(2)}) async-start(bf16[128,8,512]{0,2,1:T(8,128)(2,1)} %bitcast.125), calls=%async_computation.3 | async-start | bytes 2097152 | tf_op jit(solution)/shard_map/all_to_all | solution.py:97
  70.5 3.2 %copy-start.1 = (f32[8,4,128,512]{2,3,0,1:T(8,128)}, f32[8,4,128,512]{2,3,0,1:T(8,128)S(1)}, u32[]{:S(2)}) copy-start(f32[8,4,128,512]{2,3,0,1:T(8,128)S(1)} %get-tuple-element.32) | copy-start | bytes 25165828
  89.9 4.6 %copy-start = (bf16[8,4,128,512]{2,3,0,1:T(8,128)(2,1)S(1)}, bf16[8,4,128,512]{2,3,0,1:T(8,128)(2,1)}, u32[]{:S(2)}) copy-start(bf16[8,4,128,512]{2,3,0,1:T(8,128)(2,1)} %fusion.44) | copy-start | bytes 12582916
  105.6 23.9 %all-to-all-start.6 = ((bf16[8,64,512]{2,1,0:T(8,128)(2,1)}), bf16[8,64,512]{2,1,0:T(8,128)(2,1)}, u32[]{:S(2)}, u32[]{:S(2)}) async-start(bf16[8,64,512]{2,1,0:T(8,128)(2,1)} %convert_element_type.73), calls=%async_computation.6 | async-start | bytes 1048576 | tf_op jit(solution)/shard_map/all_to_all | solution.py:124
  128.1 24.2 %copy-start.2 = (bf16[8,128,4,128]{1,3,0,2:T(8,128)(2,1)S(1)}, bf16[8,128,4,128]{1,3,0,2:T(8,128)(2,1)}, u32[]{:S(2)}) copy-start(bf16[8,128,4,128]{1,3,0,2:T(8,128)(2,1)} %get-tuple-element.22) | copy-start | bytes 3145732
  129.5 19.1 %all-to-all-start.5 = ((bf16[8,64,512]{2,1,0:T(8,128)(2,1)}), bf16[8,64,512]{2,1,0:T(8,128)(2,1)S(1)}, u32[]{:S(2)}, u32[]{:S(2)}) async-start(bf16[8,64,512]{2,1,0:T(8,128)(2,1)} %convert_element_type.70), calls=%async_computation.5 | async-start | bytes 1048576 | tf_op jit(solution)/shard_map/all_to_all | solution.py:121
  148.6 28.9 %all-to-all-start.4 = ((bf16[8,128,512]{1,2,0:T(8,128)(2,1)}), bf16[8,128,512]{1,2,0:T(8,128)(2,1)S(1)}, u32[]{:S(2)}, u32[]{:S(2)}) async-start(bf16[8,128,512]{1,2,0:T(8,128)(2,1)} %bitcast.28), calls=%async_computation.4 | async-start | bytes 2097152 | tf_op jit(solution)/shard_map/all_to_all | solution.py:118
  177.6 54.6 %all-to-all-start.2 = ((bf16[8,128,512]{1,2,0:T(8,128)(2,1)}), bf16[8,128,512]{1,2,0:T(8,128)(2,1)S(1)}, u32[]{:S(2)}, u32[]{:S(2)}) async-start(bf16[8,128,512]{1,2,0:T(8,128)(2,1)} %bitcast.18), calls=%async_computation.2 | async-start | bytes 2097152 | tf_op jit(solution)/shard_map/all_to_all | solution.py:117
